TPU v7x, 256 devices: a whole 4x4x8 slice. The times are simulated.
256 devices in a mesh: expert: 64 (over y, z, core), dp: 4 (over x).
Axes of the slice: x: 4, y: 4, z: 8, core: 2. Of those that a mesh axis runs over, the one named last changes fastest.
Arguments:
- grad_rows: bfloat16 [4, 32768, 2048], P('dp', 'expert'), may hold values from -6 to 6
- counts: int32 [4, 64, 64], P('dp', 'expert'), may hold values from 0 to 10, as said below
- order: int32 [4, 32768], P('dp', 'expert'), may hold values from 0 to 511, as said below
- hidden: bfloat16 [4, 64, 640, 768], P('dp', 'expert'), may hold values from -0.29882812 to 0.29882812
- down_weight: bfloat16 [64, 768, 2048], P('expert'), may hold values from -0.21875 to 0.21875
- error_in: bfloat16 [4, 64, 768, 2048], P('dp', 'expert'), may hold values from -6 to 6
- q_init: bfloat16 [64, 2048, 64], P('expert'), may hold values from -6 to 6
Outputs:
- input_grad: bfloat16 [4, 32768, 768], P('dp', 'expert')
- p_basis: float32 [64, 768, 64], P('expert')
- q_factor: float32 [64, 2048, 64], P('expert')
- error_out: bfloat16 [4, 64, 768, 2048], P('dp', 'expert')
Inputs may be any that keep to these rules, and one draw needn't show every extreme that they name: On each device (r, s) the 64 counts sum to 512; in every draw one expert receives exactly 10 rows from every device. `order`: each device's 512 entries are a permutation of 0 to 511.
All inputs are finite; a program needn't handle non-finite values.
Results may differ from a plain program's by a relative error of at most 0.001.
Values may be sent and summed in bfloat16 or wider, within the bound.
A program may use at most 128 MiB of HBM per device.

v0:
```python
import jax
import jax.numpy as jnp
from jax import lax
from jax.sharding import PartitionSpec as P


def orthonormal_rows(p_rows, gram):
    lower = jnp.linalg.cholesky(gram)
    return lax.linalg.triangular_solve(lower, p_rows, left_side=False, lower=True, transpose_a=True)


def shards(grad_rows, counts, order, hidden, down_weight, error_in, q_init):
    local_rows = grad_rows[0]
    route_count = counts[0, 0]
    order_local = order[0]
    experts = route_count.shape[0]
    total_rows = local_rows.shape[0]
    width = local_rows.shape[1]
    saved_hidden = hidden[0, 0]
    hidden_units = saved_hidden.shape[1]
    capacity = saved_hidden.shape[0] // experts
    expert_weight = down_weight[0]
    route_ends = jnp.cumsum(route_count)
    route_starts = route_ends - route_count
    slot_ids = jnp.arange(capacity, dtype=jnp.int32)
    pick_index = jnp.minimum(route_starts[:, None] + slot_ids[None, :], total_rows - 1)
    slot_valid = slot_ids[None, :] < route_count[:, None]
    outgoing = local_rows[pick_index.reshape(-1)].reshape(experts, capacity, width)
    outgoing = jnp.where(slot_valid[:, :, None], outgoing, jnp.zeros((), jnp.bfloat16))
    arrived = lax.all_to_all(outgoing, "expert", split_axis=0, concat_axis=0, tiled=True)
    returned = lax.all_to_all(
        jnp.einsum(
            "ncd,fd->ncf", arrived, expert_weight, preferred_element_type=jnp.float32
        ).astype(jnp.bfloat16),
        "expert",
        split_axis=0,
        concat_axis=0,
        tiled=True,
    )
    arrived_flat = arrived.reshape(experts * capacity, width)
    grad_w = lax.dot_general(
        saved_hidden, arrived_flat, (((0,), (0,)), ((), ())), preferred_element_type=jnp.float32
    )
    moment = grad_w + error_in[0, 0].astype(jnp.float32)
    q_start = q_init[0].astype(jnp.float32)
    partial_p = jnp.dot(moment, q_start, precision=lax.Precision.HIGHEST)
    p_total = lax.psum(partial_p, "dp")
    p_basis = orthonormal_rows(
        p_total, jnp.dot(p_total.T, p_total, precision=lax.Precision.HIGHEST)
    )
    partial_q = lax.dot_general(
        moment, p_basis, (((0,), (0,)), ((), ())), precision=lax.Precision.HIGHEST
    )
    replicas = lax.axis_size("dp")
    q_factor = lax.psum(partial_q, "dp") / replicas
    approximation = jnp.dot(p_basis, q_factor.T, precision=lax.Precision.HIGHEST)
    error_new = (moment - approximation).astype(jnp.bfloat16)
    returned_flat = returned.reshape(experts * capacity, hidden_units)
    expert_of = jnp.sum((route_ends[None, :] <= order_local[:, None]).astype(jnp.int32), axis=1)
    expert_ids = jnp.arange(experts, dtype=jnp.int32)
    onehot = (expert_of[:, None] == expert_ids[None, :]).astype(jnp.int32)
    row_base = jnp.sum(onehot * (expert_ids * capacity - route_starts)[None, :], axis=1)
    position = row_base + order_local
    input_grad = returned_flat[position]
    return (input_grad[None], p_basis[None], q_factor[None], error_new[None, None])


def solution(mesh):
    placed = (
        P("dp", "expert", None),
        P("dp", "expert", None),
        P("dp", "expert"),
        P("dp", "expert", None, None),
        P("expert", None, None),
        P("dp", "expert", None, None),
        P("expert", None, None),
    )
    return jax.shard_map(
        shards,
        mesh=mesh,
        in_specs=placed,
        out_specs=(
            P("dp", "expert", None),
            P("expert", None, None),
            P("expert", None, None),
            P("dp", "expert", None, None),
        ),
        check_vma=False,
    )
```

profile of v0, /device:TPU:1, one launch (start us, length us, event | category | flops | bytes accessed | tf_op | source)
XLA Modules:
  0.0 299.0 jit_solution(14025516916071478414)
XLA Ops:
  7.2 0.0 copy-start
  7.2 0.9 iota_compare_fusion.3
  8.1 0.8 copy.31
  8.9 0.1 reduce-window.7
  9.0 0.1 reduce.6
  9.1 0.7 multiply_subtract_fusion
  9.8 0.1 add_minimum_fusion
  9.8 0.1 min.19
  10.0 8.8 %gather_fusion = bf16[640,2048]{1,0:T(8,128)(2,1)} fusion(bf16[512,2048]{1,0:T(8,128)(2,1)} %bitcast.52, s32[1024]{0:T(1024)S(1)} %pad_clamp_fusion.1), kind=kCustom, calls=%fused_computation | custom fusion | bytes 5245440 | tf_op jit(solution)/shard_map/gather | solution.py:28
  18.8 5.4 %reshape.154 = bf16[64,10,2048]{2,1,0:T(8,128)(2,1)} reshape(bf16[640,2048]{1,0:T(8,128)(2,1)} %gather_fusion) | data formatting | bytes 5242880 | tf_op jit(solution)/shard_map/reshape | solution.py:28
  24.2 4.5 %broadcast_select_fusion = bf16[64,10,2048]{2,1,0:T(8,128)(2,1)} fusion(bf16[64,10,2048]{2,1,0:T(8,128)(2,1)} %reshape.154, pred[64,10]{1,0:T(8,128)(4,1)S(1)} %iota_compare_fusion.3), kind=kLoop, calls=%fused_computation.4 | loop fusion | flops 1310720 | bytes 5243520 | tf_op jit(solution)/shard_map/jit(_where)/select_n | solution.py:29
  28.6 13.3 %all-to-all-start = ((bf16[64,10,2048]{2,1,0:T(8,128)(2,1)}), bf16[64,10,2048]{2,1,0:T(8,128)(2,1)}, u32[]{:S(2)}, u32[]{:S(2)}) async-start(bf16[64,10,2048]{2,1,0:T(8,128)(2,1)} %broadcast_select_fusion), calls=%async_computation | async-start | bytes 8388608 | tf_op jit(solution)/shard_map/all_to_all | solution.py:30
  42.0 0.2 all-reduce.3.cloned.1.call-start
  42.2 4.6 %copy.34 = bf16[1,1,768,2048]{2,3,1,0:T(8,128)(2,1)} copy(bf16[1,1,768,2048]{3,2,1,0:T(8,128)(2,1)} %param.12) | data formatting | bytes 6291456 | tf_op args[5]
  46.9 91.0 %all-to-all-done = bf16[64,10,2048]{2,1,0:T(8,128)(2,1)} async-done(((bf16[64,10,2048]{2,1,0:T(8,128)(2,1)}), bf16[64,10,2048]{2,1,0:T(8,128)(2,1)}, u32[]{:S(2)}, u32[]{:S(2)}) %all-to-all-start) | async-done | bytes 2621472 | tf_op jit(solution)/shard_map/all_to_all | solution.py:30
  137.9 5.5 %reshape.156 = bf16[640,2048]{1,0:T(8,128)(2,1)} reshape(bf16[64,10,2048]{2,1,0:T(8,128)(2,1)} %all-to-all-done) | data formatting | bytes 5242880 | tf_op jit(solution)/shard_map/reshape | solution.py:40
  143.4 0.0 copy-start.3
  143.4 5.8 %convert_add_fusion = f32[768,2048]{0,1:T(8,128)S(1)} fusion(bf16[640,2048]{1,0:T(8,128)(2,1)} %reshape.156, bf16[1,1,768,2048]{2,3,1,0:T(8,128)(2,1)} %copy.34, bf16[1,1,640,768]{3,2,1,0:T(8,128)(2,1)} %param.10), kind=kOutput, calls=%fused_computation.2 | convolution fusion | flops 2016411648 | bytes 13041664 | tf_op jit(solution)/shard_map/dot_general | solution.py:41
  149.2 0.0 copy-start.1
  149.2 2.7 copy-done.1
  151.9 0.0 copy-done.3
  151.9 3.2 %fusion.11 = f32[768,64]{0,1:T(8,128)} fusion(f32[768,2048]{0,1:T(8,128)S(1)} %convert_add_fusion, bf16[1,2048,64]{1,2,0:T(8,128)(2,1)S(1)} %copy-done.3), kind=kOutput, calls=%fused_computation.13 | convolution fusion | flops 1207959552 | bytes 6750208 | tf_op jit(solution)/shard_map/dot_general | solution.py:46
  155.0 0.0 all-reduce.3.cloned.1.call-update
  155.1 0.0 copy-done
  155.1 7.0 %fusion.4 = bf16[64,10,768]{2,0,1:T(8,128)(2,1)S(1)} fusion(bf16[1,768,2048]{2,1,0:T(8,128)(2,1)S(1)} %copy-done, bf16[64,10,2048]{2,1,0:T(8,128)(2,1)} %all-to-all-done), kind=kOutput, calls=%fused_computation.9 | convolution fusion | flops 2013757440 | bytes 6750208 | tf_op jit(solution)/shard_map/ncd,fd->ncf/dot_general | solution.py:32
  162.0 1.7 copy.33
  163.7 5.9 %all-to-all-start.1 = ((bf16[64,10,768]{2,1,0:T(8,128)(2,1)}), bf16[64,10,768]{2,1,0:T(8,128)(2,1)}, u32[]{:S(2)}, u32[]{:S(2)}) async-start(bf16[64,10,768]{2,1,0:T(8,128)(2,1)} %copy.33), calls=%async_computation.1 | async-start | bytes 3145728 | tf_op jit(solution)/shard_map/all_to_all | solution.py:31
  169.6 0.3 all-reduce.5.cloned.1.call-start
  169.9 27.0 %all-reduce.3.cloned.1.call-done = f32[768,64]{0,1:T(8,128)} async-done(((f32[768,64]{0,1:T(8,128)}), f32[768,64]{0,1:T(8,128)}) %all-reduce.3.cloned.1.call-update) | async-done | bytes 196624 | tf_op jit(solution)/shard_map/psum | solution.py:47
  196.9 1.3 fusion.20
  198.3 0.1 copy.35
  198.4 5.8 %cholesky.16 = f32[64,64]{1,0:T(8,128)S(1)} custom-call(f32[64,64]{1,0:T(8,128)S(1)} %fusion.17), custom_call_target="Cholesky" | custom-call | tf_op jit(solution)/shard_map/jit(cholesky)/cholesky | solution.py:8
  204.2 0.6 compare_reduce_fusion
  204.9 0.7 fusion.14
  205.5 4.9 %custom-call.6 = f32[1,64,64]{1,2,0:T(8,128)S(1)} custom-call(f32[1,64,64]{2,1,0:T(8,128)S(1)} %fusion.14), custom_call_target="InvertDiagBlocksLowerTriangular" | custom-call | tf_op jit(solution)/shard_map/triangular_solve | solution.py:9
  210.4 1.3 fusion.15
  211.7 0.0 copy-start.2
  211.8 0.0 copy-start.4
  211.8 9.8 %fusion.21 = f32[2048,64]{0,1:T(8,128)} fusion(f32[768,2048]{0,1:T(8,128)} %copy-done.1, f32[768,64]{0,1:T(8,128)S(1)} %fusion.15), kind=kOutput, calls=%fused_computation.41 | convolution fusion | flops 1207959552 | bytes 7012352 | tf_op jit(solution)/shard_map/dot_general | solution.py:51
  221.6 0.0 all-reduce.5.cloned.1.call-update
  221.6 0.0 copy-done.4
  221.6 0.1 convert_reduce_fusion
  221.7 0.1 select_reduce_fusion
  221.8 47.9 %all-reduce.5.cloned.1.call-done = f32[2048,64]{0,1:T(8,128)} async-done(((f32[2048,64]{0,1:T(8,128)}), f32[2048,64]{0,1:T(8,128)}) %all-reduce.5.cloned.1.call-update) | async-done | bytes 524304 | tf_op jit(solution)/shard_map/psum | solution.py:55
  269.8 0.0 copy-done.2
  269.8 8.5 %fusion.2 = bf16[1,1,768,2048]{2,3,1,0:T(8,128)(2,1)} fusion(f32[768,2048]{0,1:T(8,128)} %copy-done.1, f32[768,64]{0,1:T(8,128)S(1)} %fusion.15, f32[2048,64]{0,1:T(8,128)} %all-reduce.5.cloned.1.call-done), kind=kOutput, calls=%fused_computation.7 | convolution fusion | flops 1211236352 | bytes 10158080 | tf_op jit(solution)/shard_map/dot_general | solution.py:56
  278.2 4.6 %copy.37 = bf16[1,1,768,2048]{3,2,1,0:T(8,128)(2,1)} copy(bf16[1,1,768,2048]{2,3,1,0:T(8,128)(2,1)} %fusion.2) | data formatting | bytes 6291456
  282.9 1.9 multiply_bitcast_fusion
  284.7 0.0 all-to-all-done.1
  284.7 3.0 %reshape.155 = bf16[640,768]{1,0:T(8,128)(2,1)} reshape(bf16[64,10,768]{2,1,0:T(8,128)(2,1)} %all-to-all-done.1) | data formatting | bytes 1966080 | tf_op jit(solution)/shard_map/reshape | solution.py:58
  287.8 4.4 %gather_fusion.1 = bf16[512,768]{1,0:T(8,128)(2,1)} fusion(bf16[640,768]{1,0:T(8,128)(2,1)} %reshape.155, s32[1024]{0:T(1024)S(1)} %pad_clamp_fusion), kind=kCustom, calls=%fused_computation.1 | custom fusion | bytes 1574912 | tf_op jit(solution)/shard_map/gather | solution.py:64
  (6 shorter events, 0.1 us)
Async XLA Ops:
  7.2 147.9 %copy-start = (bf16[1,768,2048]{2,1,0:T(8,128)(2,1)S(1)}, bf16[1,768,2048]{2,1,0:T(8,128)(2,1)}, u32[]{:S(2)}) copy-start(bf16[1,768,2048]{2,1,0:T(8,128)(2,1)} %param.11) | copy-start | bytes 9437188
  28.6 109.2 %all-to-all-start = ((bf16[64,10,2048]{2,1,0:T(8,128)(2,1)}), bf16[64,10,2048]{2,1,0:T(8,128)(2,1)}, u32[]{:S(2)}, u32[]{:S(2)}) async-start(bf16[64,10,2048]{2,1,0:T(8,128)(2,1)} %broadcast_select_fusion), calls=%async_computation | async-start | bytes 8388608 | tf_op jit(solution)/shard_map/all_to_all | solution.py:30
  42.0 154.9 %all-reduce.3.cloned.1.call-start = ((), (), s32[]{:S(2)}) async-start(), calls=%async_computation.2 | async-start | bytes 393216 | tf_op jit(solution)/shard_map/psum | solution.py:47
  143.4 8.5 %copy-start.3 = (bf16[1,2048,64]{1,2,0:T(8,128)(2,1)S(1)}, bf16[1,2048,64]{1,2,0:T(8,128)(2,1)}, u32[]{:S(2)}) copy-start(bf16[1,2048,64]{1,2,0:T(8,128)(2,1)} %param.13) | copy-start | bytes 786436
  149.2 2.7 copy-start.1
  163.7 121.0 %all-to-all-start.1 = ((bf16[64,10,768]{2,1,0:T(8,128)(2,1)}), bf16[64,10,768]{2,1,0:T(8,128)(2,1)}, u32[]{:S(2)}, u32[]{:S(2)}) async-start(bf16[64,10,768]{2,1,0:T(8,128)(2,1)} %copy.33), calls=%async_computation.1 | async-start | bytes 3145728 | tf_op jit(solution)/shard_map/all_to_all | solution.py:31
  169.6 100.1 %all-reduce.5.cloned.1.call-start = ((), (), s32[]{:S(2)}) async-start(), calls=%async_computation.3 | async-start | bytes 1048576 | tf_op jit(solution)/shard_map/psum | solution.py:55
  211.7 58.0 %copy-start.2 = (f32[768,64]{0,1:T(8,128)}, f32[768,64]{0,1:T(8,128)S(1)}, u32[]{:S(2)}) copy-start(f32[768,64]{0,1:T(8,128)S(1)} %fusion.15) | copy-start | bytes 589828
  211.8 9.9 %copy-start.4 = (s32[1,512]{1,0:T(1,128)S(1)}, s32[1,512]{1,0:T(1,128)}, u32[]{:S(2)}) copy-start(s32[1,512]{1,0:T(1,128)} %param.9) | copy-start | bytes 6148
Sparse Core Ops, SparseCore 0:
  155.2 41.7 all-reduce.2
  221.7 47.9 all-reduce.4
where the time goes:
time: 301 us; the launch traced here: 299 us
  waiting for transfers between devices  166 us (55%)
  local copies, waits for them, and re-layouts  41.8 us (14%)
  matrix products  36.8 us (12%)
  other arithmetic  20.5 us (7%)
  starting transfers between devices  19.7 us (7%)
  between operations  14.2 us (5%)
    all_to_all x1, waiting for transfers between devices, shards(): lax.all_to_all(outgoing, 'expert', split_axis=0, concat_axis=0, tiled=True)  91 us
    psum x1, waiting for transfers between devices, shards(): q_factor = lax.psum(partial_q, 'dp') / replicas  47.9 us
    psum x1, waiting for transfers between devices, shards(): p_total = lax.psum(partial_p, 'dp')  27 us
    all_to_all x1, starting transfers between devices, shards(): lax.all_to_all(outgoing, 'expert', split_axis=0, concat_axis=0, tiled=True)  13.3 us
    unnamed x12, local copies, waits for them, and re-layouts  11.9 us
    dot_general x1, matrix products, shards(): lax.dot_general(moment, p_basis, (((0,), (0,)), ((), ())), precision=lax....  9.82 us
    gather x1, local copies, waits for them, and re-layouts, shards(): local_rows[pick_index.reshape(-1)].reshape(experts, capacity, width)  8.78 us
    dot_general x1, matrix products, shards(): jnp.dot(p_basis, q_factor.T, precision=lax.Precision.HIGHEST)  8.46 us
  transfers between devices with their start and end apart: 4, of which 3 were waited for; matrix products, arithmetic and copies ran while one was open for 18% of the time, Pallas kernels for 0%

commit v1 on v0

v1 whole, which is shorter than its diff:
```python
import jax
import jax.numpy as jnp
from jax import lax
from jax.experimental import pallas as pl
from jax.experimental.pallas import tpu as pltpu
from jax.sharding import PartitionSpec as P

MESH = pl.DeviceIdType.MESH
F32 = jnp.float32
BF16 = jnp.bfloat16

NY, NZ, NC, NDP = 4, 8, 2, 4
ROWS, D, FF, RANK, EXPERTS = 512, 2048, 768, 64, 64
GROUPS, MEMBERS = 8, 8
GROUP_ROWS = 80
WIDE = D + 512
BACK = FF + 256
BLOCK = D // NDP
P_ROWS = RANK // NDP


def nn(a, b, precision=None):
    return lax.dot_general(
        a, b, (((1,), (0,)), ((), ())), precision=precision, preferred_element_type=F32
    )


def nt(a, b, precision=None):
    return lax.dot_general(
        a, b, (((1,), (1,)), ((), ())), precision=precision, preferred_element_type=F32
    )


def split(a):
    high = a.astype(BF16)
    return high, (a - high.astype(F32)).astype(BF16)


def onehot(mask):
    return jnp.where(mask, 1.0, 0.0).astype(BF16)


def iota(shape, axis):
    return lax.broadcasted_iota(jnp.int32, shape, axis)


def z_step(k):
    half = (k + 1) // 2
    return 4 + (1 - 2 * (k % 2)) * half


def shift(y, z, c, k, m, sign):
    there_y = (y + sign * (m // 2) + NY) % NY
    there_z = (z + sign * z_step(k) + NZ) % NZ
    there_c = (c + m % 2) % NC
    return (there_y * NZ + there_z) * NC + there_c


def group_codes(y, z, c, k, sign, scale):
    main = iota((64, 1), 0)
    tail = iota((16, 1), 0)
    main_code = shift(y, z, c, k, main // 8, sign) * scale + main % 8
    tail_code = shift(y, z, c, k, tail // 2, sign) * scale + 8 + tail % 2
    return main_code, tail_code


def routes(ends, rows):
    passed = ends <= rows
    expert = jnp.sum(jnp.where(passed, 1.0, 0.0), axis=0, keepdims=True)
    start = jnp.max(jnp.where(passed, ends, 0.0), axis=0, keepdims=True)
    return expert * 16.0 + (rows - start)


def inverse_factor(gram):
    lanes = iota((RANK, 2 * RANK), 1)
    rows = iota((RANK, 2 * RANK), 0)
    work = jnp.concatenate([gram, jnp.where(iota((RANK, RANK), 0) == iota((RANK, RANK), 1), 1.0, 0.0)], axis=1)
    blocks = [work[8 * b : 8 * b + 8] for b in range(8)]
    below = iota((8, 1), 0)
    for k in range(RANK):
        own, at = k // 8, k % 8
        row = blocks[own][at : at + 1, :]
        scaled = row / row[:, k : k + 1]
        for b in range(own, 8):
            factor = blocks[b][:, k : k + 1]
            if b == own:
                factor = jnp.where(below > at, factor, 0.0)
            blocks[b] = blocks[b] - factor * scaled
    work = jnp.concatenate(blocks, axis=0)
    pivots = jnp.sum(jnp.where(lanes == rows, work, 0.0), axis=1, keepdims=True)
    return work[:, RANK:] * lax.rsqrt(pivots)


def kernel(
    x_hbm, counts_ref, order_ref, hidden_hbm, weight_hbm, error_hbm, q_ref,
    back_out, p_out, q_out, error_out,
    x, hidden, weight, error, send, recv, held, hidden_p, hidden_t, moment, moment_h, moment_l,
    pick, back_send, back_recv, back_rows, p_part, p_recv, p_full, z_part, z_recv, q_full,
    error_new, factor_t, load_sem, store_sem, send_sem, recv_sem, back_send_sem, back_recv_sem,
    p_sem, g_sem, z_sem, q_sem, own_sem,
):
    me = lax.axis_index("expert")
    replica = lax.axis_index("dp")
    y, z, c = me // (NZ * NC), (me // NC) % NZ, me % NC

    loads = [
        pltpu.make_async_copy(src, dst, load_sem.at[i])
        for i, (src, dst) in enumerate(
            [(x_hbm, x), (hidden_hbm, hidden), (error_hbm, error), (weight_hbm, weight)]
        )
    ]
    for load in loads:
        load.start()

    barrier = pltpu.get_barrier_semaphore()

    @pl.loop(1, EXPERTS)
    def _(k):
        pl.semaphore_signal(
            barrier, inc=1, device_id={"expert": (me + k) % EXPERTS}, device_id_type=MESH
        )

    for i in range(1, NDP):
        pl.semaphore_signal(
            barrier, inc=1, device_id={"dp": (replica + i) % NDP}, device_id_type=MESH
        )

    counts = counts_ref[...].astype(F32)
    ends = jnp.sum(
        jnp.where(iota((EXPERTS, EXPERTS), 1) <= iota((EXPERTS, EXPERTS), 0), counts, 0.0),
        axis=1,
        keepdims=True,
    )
    codes = routes(ends, iota((1, ROWS), 1).astype(F32))
    loads[0].wait()

    def forward(k, m):
        return pltpu.make_async_remote_copy(
            src_ref=send.at[k, m],
            dst_ref=recv.at[k, m],
            send_sem=send_sem.at[k, m],
            recv_sem=recv_sem.at[k, m],
            device_id={"expert": shift(y, z, c, k, m, 1)},
            device_id_type=MESH,
        )

    def backward(k, m):
        return pltpu.make_async_remote_copy(
            src_ref=back_send.at[k, m],
            dst_ref=back_recv.at[k, m],
            send_sem=back_send_sem.at[k, m],
            recv_sem=back_recv_sem.at[k, m],
            device_id={"expert": shift(y, z, c, k, m, -1)},
            device_id_type=MESH,
        )

    def pack(k):
        rows = iota((64, 1), 0)
        expert = shift(y, z, c, k, rows // 8, 1) * 16
        main = onehot(codes == (expert + rows % 8).astype(F32))
        tail = codes == (expert + 8 + rows % 2).astype(F32)
        part = (rows % 8) // 2
        total = jnp.zeros((64, 512), F32)
        for i in range(4):
            columns = x[:, 512 * i : 512 * i + 512]
            both = nn(
                jnp.concatenate([main, onehot(tail & (part == i))], axis=0), columns
            )
            send[k, :, :, 512 * i : 512 * i + 512] = both[:64].reshape(8, 8, 512).astype(BF16)
            total = total + both[64:]
        send[k, :, :, D:] = total.reshape(8, 8, 512).astype(BF16)

    pack(0)
    pl.semaphore_wait(barrier, EXPERTS - 1 + NDP - 1)
    for m in range(MEMBERS):
        forward(0, m).start()

    @pl.loop(1, GROUPS - 1)
    def _(k):
        pack(k)
        for m in range(MEMBERS):
            forward(k, m).start()

    pack(GROUPS - 1)
    for m in range(1, MEMBERS):
        forward(GROUPS - 1, m).start()
    own = pltpu.make_async_copy(send.at[GROUPS - 1, 0], recv.at[GROUPS - 1, 0], own_sem.at[0])
    own.start()

    loads[1].wait()

    @pl.loop(0, GROUPS)
    def _(k):
        main_code, tail_code = group_codes(y, z, c, k, -1, 10)
        code = jnp.concatenate([main_code, tail_code], axis=0)
        rows = pl.ds(pl.multiple_of(k * GROUP_ROWS, 16), GROUP_ROWS)
        hidden_p[rows, :] = nn(onehot(iota((GROUP_ROWS, 640), 1) == code), hidden[...]).astype(BF16)

    for i in range(FF // 128):
        hidden_t[128 * i : 128 * i + 128, :] = (
            hidden_p[:, 128 * i : 128 * i + 128].astype(F32).T.astype(BF16)
        )
    wanted = routes(ends, order_ref[...].astype(F32))

    for k in range(GROUPS):
        main_code, tail_code = group_codes(y, z, c, k, 1, 16)
        code = jnp.concatenate([main_code, tail_code], axis=0).astype(F32)
        pick[k * GROUP_ROWS : (k + 1) * GROUP_ROWS, :] = onehot(wanted == code)

    q = q_ref[...]
    loads[2].wait()
    for i in range(3):
        p_part[:, 256 * i : 256 * i + 256] = nt(q, error[256 * i : 256 * i + 256, :])
    loads[3].wait()

    spread = iota((16, 64), 1)
    gathered = iota((16, 64), 0)

    def unpack(ref, k, width, parts, size):
        block = ref[k].astype(F32).reshape(64, width + size)
        main = block[:, :width].astype(BF16)
        tail = block[:, width:].astype(BF16)
        pieces = []
        for i in range(parts):
            at = (gathered // 2) * 8 + 2 * i + gathered % 2
            pieces.append(nn(onehot(spread == at), tail).astype(BF16))
        return main, jnp.concatenate(pieces, axis=1)

    def take(k):
        rows = pl.ds(pl.multiple_of(k * GROUP_ROWS, 16), GROUP_ROWS)
        main, tail = unpack(recv, k, D, 4, 512)
        mine = jnp.concatenate([main, tail], axis=0)
        held[rows, :] = mine
        high, low = split(nt(q, mine))
        both = nn(jnp.concatenate([high, low], axis=0), hidden_p[rows, :])
        p_part[...] += both[:RANK] + both[RANK:]

    def answer(k):
        rows = pl.ds(pl.multiple_of(k * GROUP_ROWS, 16), GROUP_ROWS)
        mine = held[rows, :]
        for i in range(3):
            columns = slice(256 * i, 256 * i + 256)
            slot = nt(mine, weight[columns, :])
            back_send[k, :, :, columns] = slot[:64].reshape(8, 8, 256).astype(BF16)
            tail = slot[64:].astype(BF16)
            to = iota((64, 16), 0)
            at = (to // 8) * 2 + to % 2
            mask = (iota((64, 16), 1) == at) & ((to % 8) // 2 == i)
            placed = nn(onehot(mask), tail)
            if i == 0:
                total = placed
            else:
                total = total + placed
        back_send[k, :, :, FF:] = total.reshape(8, 8, 256).astype(BF16)

    @pl.loop(0, GROUPS - 1)
    def _(k):
        for m in range(MEMBERS):
            forward(k, m).wait_recv()
        take(k)
        answer(k)

    for m in range(1, MEMBERS):
        forward(GROUPS - 1, m).wait_recv()
    own.wait()
    take(GROUPS - 1)

    def p_scatter(i):
        peer = (replica + i) % NDP
        return pltpu.make_async_remote_copy(
            src_ref=p_part.at[pl.ds(pl.multiple_of(peer * P_ROWS, 8), P_ROWS)],
            dst_ref=p_recv.at[i - 1],
            send_sem=p_sem.at[0, i - 1],
            recv_sem=p_sem.at[1, i - 1],
            device_id={"dp": peer},
            device_id_type=MESH,
        )

    my_rows = pl.ds(pl.multiple_of(replica * P_ROWS, 8), P_ROWS)

    def p_gather(i):
        return pltpu.make_async_remote_copy(
            src_ref=p_full.at[my_rows],
            dst_ref=p_full.at[my_rows],
            send_sem=g_sem.at[0, i - 1],
            recv_sem=g_sem.at[1, i - 1],
            device_id={"dp": (replica + i) % NDP},
            device_id_type=MESH,
        )

    for i in range(1, NDP):
        p_scatter(i).start()
    answer(GROUPS - 1)
    for i in range(1, NDP):
        p_scatter(i).wait_recv()
    p_full[my_rows, :] = p_part[my_rows, :] + p_recv[0] + p_recv[1] + p_recv[2]
    for i in range(1, NDP):
        p_gather(i).start()

    @pl.loop(0, GROUPS - 1)
    def _(k):
        for m in range(MEMBERS):
            backward(k, m).start()

    for m in range(1, MEMBERS):
        backward(GROUPS - 1, m).start()
    own_back = pltpu.make_async_copy(
        back_send.at[GROUPS - 1, 0], back_recv.at[GROUPS - 1, 0], own_sem.at[1]
    )
    own_back.start()

    @pl.loop(0, D // 256)
    def _(i):
        columns = pl.ds(pl.multiple_of(i * 256, 256), 256)
        value = nn(hidden_t[...], held[:, columns]) + error[:, columns].astype(F32)
        moment[:, columns] = value
        high, low = split(value)
        moment_h[:, columns] = high
        moment_l[:, columns] = low

    for i in range(1, NDP):
        p_gather(i).wait_recv()

    total = p_full[...]
    total_h, total_l = split(total)
    total_both = jnp.concatenate([total_h, total_l], axis=0)

    def z_scatter(i):
        peer = (replica + i) % NDP
        return pltpu.make_async_remote_copy(
            src_ref=z_part.at[i],
            dst_ref=z_recv.at[i - 1],
            send_sem=z_sem.at[0, i - 1],
            recv_sem=z_sem.at[1, i - 1],
            device_id={"dp": peer},
            device_id_type=MESH,
        )

    for i in (2, 1, 3, 0):
        block = pl.ds(pl.multiple_of(((replica + i) % NDP) * BLOCK, BLOCK), BLOCK)
        both = nn(total_both, moment_h[:, block])
        z_part[i] = both[:RANK] + both[RANK:] + nn(total_h, moment_l[:, block])
        if i:
            z_scatter(i).start()

    gram = nt(total, total, lax.Precision.HIGHEST)
    inverse = inverse_factor(gram)
    basis = nn(inverse, total, lax.Precision.HIGHEST)
    p_out[...] = basis
    basis_h, basis_l = split(basis)
    three = jnp.concatenate([basis_h, basis_l, basis_h], axis=0).astype(F32)
    for i in range(FF // 128):
        factor_t[128 * i : 128 * i + 128, :] = three[:, 128 * i : 128 * i + 128].T.astype(BF16)

    for i in range(1, NDP):
        z_scatter(i).wait_recv()
    z_total = z_part[0] + z_recv[0] + z_recv[1] + z_recv[2]
    q_full[replica] = nn(inverse, z_total, lax.Precision.HIGHEST) / NDP

    def q_gather(i):
        return pltpu.make_async_remote_copy(
            src_ref=q_full.at[replica],
            dst_ref=q_full.at[replica],
            send_sem=q_sem.at[0, i - 1],
            recv_sem=q_sem.at[1, i - 1],
            device_id={"dp": (replica + i) % NDP},
            device_id_type=MESH,
        )

    for i in range(1, NDP):
        q_gather(i).start()

    def store(i):
        block = pl.ds(pl.multiple_of(((replica + NDP - i) % NDP) * BLOCK, BLOCK), BLOCK)
        return pltpu.make_async_copy(error_new.at[i], error_out.at[:, block], store_sem.at[i])

    for i in (0, 1, 3, 2):
        if i:
            q_gather(i).wait_recv()
        owner = (replica + NDP - i) % NDP
        block = pl.ds(pl.multiple_of(owner * BLOCK, BLOCK), BLOCK)
        part = q_full[owner]
        q_out[:, block] = part
        part_h, part_l = split(part)
        part_three = jnp.concatenate([part_h, part_h, part_l], axis=0)
        for j in range(3):
            rows = slice(256 * j, 256 * j + 256)
            error_new[i, rows, :] = (
                moment[rows, block] - nn(factor_t[rows, :], part_three)
            ).astype(BF16)
        store(i).start()

    own_back.wait()

    @pl.loop(0, GROUPS - 1)
    def _(k):
        for m in range(MEMBERS):
            backward(k, m).wait_recv()
        rows = pl.ds(pl.multiple_of(k * GROUP_ROWS, 16), GROUP_ROWS)
        main, tail = unpack(back_recv, k, FF, 3, 256)
        back_rows[rows, :] = jnp.concatenate([main, tail], axis=0)

    for m in range(1, MEMBERS):
        backward(GROUPS - 1, m).wait_recv()
    main, tail = unpack(back_recv, GROUPS - 1, FF, 3, 256)
    back_rows[(GROUPS - 1) * GROUP_ROWS :, :] = jnp.concatenate([main, tail], axis=0)
    for i in range(4):
        chosen = lax.dot_general(
            pick[:, 128 * i : 128 * i + 128],
            back_rows[...],
            (((0,), (0,)), ((), ())),
            preferred_element_type=F32,
        )
        back_out[128 * i : 128 * i + 128, :] = chosen.astype(BF16)

    for i in range(NDP):
        store(i).wait()
    for i in range(1, NDP):
        p_scatter(i).wait_send()
        p_gather(i).wait_send()
        z_scatter(i).wait_send()
        q_gather(i).wait_send()

    @pl.loop(0, GROUPS - 1)
    def _(k):
        for m in range(MEMBERS):
            forward(k, m).wait_send()
            backward(k, m).wait_send()

    for m in range(1, MEMBERS):
        forward(GROUPS - 1, m).wait_send()
        backward(GROUPS - 1, m).wait_send()


def shards(grad_rows, counts, order, hidden, down_weight, error_in, q_init):
    anywhere = pl.BlockSpec(memory_space=pl.ANY)
    vmem = pl.BlockSpec(memory_space=pltpu.VMEM)
    dma = pltpu.SemaphoreType.DMA
    back, basis, factor, error_new = pl.pallas_call(
        kernel,
        out_shape=(
            jax.ShapeDtypeStruct((ROWS, FF), BF16),
            jax.ShapeDtypeStruct((RANK, FF), F32),
            jax.ShapeDtypeStruct((RANK, D), F32),
            jax.ShapeDtypeStruct((FF, D), BF16),
        ),
        in_specs=[anywhere, vmem, vmem, anywhere, anywhere, anywhere, vmem],
        out_specs=(vmem, vmem, vmem, anywhere),
        scratch_shapes=[
            pltpu.VMEM((ROWS, D), BF16),
            pltpu.VMEM((640, FF), BF16),
            pltpu.VMEM((FF, D), BF16),
            pltpu.VMEM((FF, D), BF16),
            pltpu.VMEM((GROUPS, MEMBERS, 8, WIDE), BF16),
            pltpu.VMEM((GROUPS, MEMBERS, 8, WIDE), BF16),
            pltpu.VMEM((640, D), BF16),
            pltpu.VMEM((640, FF), BF16),
            pltpu.VMEM((FF, 640), BF16),
            pltpu.VMEM((FF, D), F32),
            pltpu.VMEM((FF, D), BF16),
            pltpu.VMEM((FF, D), BF16),
            pltpu.VMEM((640, ROWS), BF16),
            pltpu.VMEM((GROUPS, MEMBERS, 8, BACK), BF16),
            pltpu.VMEM((GROUPS, MEMBERS, 8, BACK), BF16),
            pltpu.VMEM((640, FF), BF16),
            pltpu.VMEM((RANK, FF), F32),
            pltpu.VMEM((NDP - 1, P_ROWS, FF), F32),
            pltpu.VMEM((RANK, FF), F32),
            pltpu.VMEM((NDP, RANK, BLOCK), F32),
            pltpu.VMEM((NDP - 1, RANK, BLOCK), F32),
            pltpu.VMEM((NDP, RANK, BLOCK), F32),
            pltpu.VMEM((NDP, FF, BLOCK), BF16),
            pltpu.VMEM((FF, 3 * RANK), BF16),
            dma((4,)),
            dma((NDP,)),
            dma((GROUPS, MEMBERS)),
            dma((GROUPS, MEMBERS)),
            dma((GROUPS, MEMBERS)),
            dma((GROUPS, MEMBERS)),
            dma((2, NDP - 1)),
            dma((2, NDP - 1)),
            dma((2, NDP - 1)),
            dma((2, NDP - 1)),
            dma((2,)),
        ],
        compiler_params=pltpu.CompilerParams(
            collective_id=0, has_side_effects=True, vmem_limit_bytes=58 << 20
        ),
        name="routed_backward",
    )(
        grad_rows[0],
        counts[0],
        order,
        hidden[0, 0],
        down_weight[0],
        error_in[0, 0],
        q_init[0].T,
    )
    return back[None], basis.T[None], factor.T[None], error_new[None, None]


def solution(mesh):
    placed = (
        P("dp", "expert", None),
        P("dp", "expert", None),
        P("dp", "expert"),
        P("dp", "expert", None, None),
        P("expert", None, None),
        P("dp", "expert", None, None),
        P("expert", None, None),
    )
    return jax.shard_map(
        shards,
        mesh=mesh,
        in_specs=placed,
        out_specs=(
            P("dp", "expert", None),
            P("expert", None, None),
            P("expert", None, None),
            P("dp", "expert", None, None),
        ),
        check_vma=False,
    )
```

time: 301 us -> 126 us (0.42)
  waiting for transfers between devices: 166 us -> 0 us
  Pallas kernels: 0 us -> 115 us
  matrix products: 36.8 us -> 0 us
  local copies, waits for them, and re-layouts: 41.8 us -> 9.52 us
  other arithmetic: 20.5 us -> 0 us
  starting transfers between devices: 19.7 us -> 0 us
  between operations: 14.2 us -> 0.64 us
    pallas_call x0 -> x1, Pallas kernels: none -> 115 us  [shards(): pl.pallas_call(kernel, out_shape=(jax.ShapeDtypeStruct((ROWS, FF), BF16),...]
    all_to_all x2 -> x0, waiting for transfers between devices: 91 us -> none  [the longest x1 91 us: shards(): lax.all_to_all(outgoing, 'expert', split_axis=0, concat_axis=0, tiled=True)]
    psum x2 -> x0, waiting for transfers between devices: 74.9 us -> none  [the longest x1 47.9 us: shards(): q_factor = lax.psum(partial_q, 'dp') / replicas]
    dot_general x6 -> x0, matrix products: 35.5 us -> none  [the longest x1 9.82 us: shards(): lax.dot_general(moment, p_basis, (((0,), (0,)), ((), ())), precision=lax....]
    all_to_all x2 -> x0, starting transfers between devices: 19.3 us -> none  [the longest x1 13.3 us: shards(): lax.all_to_all(outgoing, 'expert', split_axis=0, concat_axis=0, tiled=True)]
    reshape x3 -> x0, local copies, waits for them, and re-layouts: 13.9 us -> none  [the longest x1 5.53 us: shards(): arrived_flat = arrived.reshape(experts * capacity, width)]
    gather x2 -> x0, local copies, waits for them, and re-layouts: 13.2 us -> none  [the longest x1 8.78 us: shards(): local_rows[pick_index.reshape(-1)].reshape(experts, capacity, width)]
    another operation x7 -> x0, other arithmetic: 12.3 us -> none  [the longest x3 6.52 us: orthonormal_rows(): lower = jnp.linalg.cholesky(gram)]
  transfers between devices with their start and end apart: 4 -> 0, of which waited for: 3 -> 0; matrix products, arithmetic and copies ran while one was open for 18% -> 0% of each run, Pallas kernels for 0% -> 0%
where the time goes in v1:
time: 126 us; the launch traced here: 125 us
  Pallas kernels  115 us (91%)
  local copies, waits for them, and re-layouts  9.52 us (8%)
    pallas_call x1, Pallas kernels, shards(): pl.pallas_call(kernel, out_shape=(jax.ShapeDtypeStruct((ROWS, FF), BF16),...  115 us
    unnamed x4, local copies, waits for them, and re-layouts  9.52 us

profile of v1, /device:TPU:1, one launch (start us, length us, event | category | flops | bytes accessed | tf_op | source)
XLA Modules:
  0.0 125.3 jit_solution(17238548838496010292)
XLA Ops:
  0.6 115.1 %routed_backward.1 = (bf16[512,768]{1,0:T(8,128)(2,1)}, f32[64,768]{1,0:T(8,128)}, f32[64,2048]{1,0:T(8,128)}, bf16[768,2048]{1,0:T(8,128)(2,1)}) custom-call(bf16[512,2048]{1,0:T(8,128)(2,1)} %bitcast.19, s32[1,64]{1,0:T(1,128)} %bitcast.25, s32[1,512]{1,0:T(1,128)} %order_ref.1, bf16[640,768]{1,0:T(8,128)(2,1)} %bitcast.20, bf16[768,2048]{1,0:T(8,128)(2,1)} %bitcast.17, ...), custom_call_target="tpu_custom_call" | custom-call | tf_op jit(solution)/shard_map/routed_backward/pallas_call | solution.py:439
  115.8 2.1 %copy.15 = bf16[1,512,768]{2,1,0:T(8,128)(2,1)} copy(bf16[1,512,768]{2,1,0:T(8,128)(2,1)} %bitcast.21) | data formatting | bytes 1572864
  117.8 1.6 %copy.16 = f32[1,768,64]{1,2,0:T(8,128)} copy(f32[1,768,64]{1,2,0:T(8,128)} %bitcast.24) | data formatting | bytes 393216
  119.5 1.9 %copy.17 = f32[1,2048,64]{1,2,0:T(8,128)} copy(f32[1,2048,64]{1,2,0:T(8,128)} %bitcast.22) | data formatting | bytes 1048576
  121.3 4.0 %copy.18 = bf16[1,1,768,2048]{3,2,1,0:T(8,128)(2,1)} copy(bf16[1,1,768,2048]{3,2,1,0:T(8,128)(2,1)} %bitcast.16) | data formatting | bytes 6291456

commit v2 on v1

--- a/solution.py
+++ b/solution.py
@@ -44,15 +44,15 @@
     return lax.broadcasted_iota(jnp.int32, shape, axis)
 
 
-def z_step(k):
-    half = (k + 1) // 2
-    return 4 + (1 - 2 * (k % 2)) * half
+def z_step(m):
+    half = (m + 1) // 2
+    return 4 + (1 - 2 * (m % 2)) * half
 
 
 def shift(y, z, c, k, m, sign):
-    there_y = (y + sign * (m // 2) + NY) % NY
-    there_z = (z + sign * z_step(k) + NZ) % NZ
-    there_c = (c + m % 2) % NC
+    there_y = (y + sign * ((k // 2 + m + 2) % NY) + NY) % NY
+    there_z = (z + sign * z_step(m) + NZ) % NZ
+    there_c = (c + k + 1) % NC
     return (there_y * NZ + there_z) * NC + there_c
 
 
@@ -93,10 +93,9 @@
 
 def kernel(
     x_hbm, counts_ref, order_ref, hidden_hbm, weight_hbm, error_hbm, q_ref,
-    back_out, p_out, q_out, error_out,
+    back_rows, p_out, q_full, moment_out, pick_out, factor_out,
     x, hidden, weight, error, send, recv, held, hidden_p, hidden_t, moment, moment_h, moment_l,
-    pick, back_send, back_recv, back_rows, p_part, p_recv, p_full, z_part, z_recv, q_full,
-    error_new, factor_t, load_sem, store_sem, send_sem, recv_sem, back_send_sem, back_recv_sem,
+    pick, back_send, back_recv, p_part, p_recv, p_full, z_part, z_recv, factor_t, load_sem, store_sem, send_sem, recv_sem, back_send_sem, back_recv_sem,
     p_sem, g_sem, z_sem, q_sem, own_sem,
 ):
     me = lax.axis_index("expert")
@@ -182,9 +181,9 @@
             forward(k, m).start()
 
     pack(GROUPS - 1)
-    for m in range(1, MEMBERS):
+    for m in range(MEMBERS - 1):
         forward(GROUPS - 1, m).start()
-    own = pltpu.make_async_copy(send.at[GROUPS - 1, 0], recv.at[GROUPS - 1, 0], own_sem.at[0])
+    own = pltpu.make_async_copy(send.at[GROUPS - 1, MEMBERS - 1], recv.at[GROUPS - 1, MEMBERS - 1], own_sem.at[0])
     own.start()
 
     loads[1].wait()
@@ -206,6 +205,13 @@
         main_code, tail_code = group_codes(y, z, c, k, 1, 16)
         code = jnp.concatenate([main_code, tail_code], axis=0).astype(F32)
         pick[k * GROUP_ROWS : (k + 1) * GROUP_ROWS, :] = onehot(wanted == code)
+    stores = [
+        pltpu.make_async_copy(src, dst, store_sem.at[i])
+        for i, (src, dst) in enumerate(
+            [(pick, pick_out), (moment, moment_out), (factor_t, factor_out)]
+        )
+    ]
+    stores[0].start()
 
     q = q_ref[...]
     loads[2].wait()
@@ -260,7 +266,7 @@
         take(k)
         answer(k)
 
-    for m in range(1, MEMBERS):
+    for m in range(MEMBERS - 1):
         forward(GROUPS - 1, m).wait_recv()
     own.wait()
     take(GROUPS - 1)
@@ -290,24 +296,26 @@
 
     for i in range(1, NDP):
         p_scatter(i).start()
+
+    @pl.loop(0, GROUPS - 1)
+    def _(k):
+        for m in range(MEMBERS):
+            backward(k, m).start()
+
     answer(GROUPS - 1)
+    for m in range(MEMBERS - 1):
+        backward(GROUPS - 1, m).start()
+    own_back = pltpu.make_async_copy(
+        back_send.at[GROUPS - 1, MEMBERS - 1],
+        back_recv.at[GROUPS - 1, MEMBERS - 1],
+        own_sem.at[1],
+    )
+    own_back.start()
     for i in range(1, NDP):
         p_scatter(i).wait_recv()
     p_full[my_rows, :] = p_part[my_rows, :] + p_recv[0] + p_recv[1] + p_recv[2]
     for i in range(1, NDP):
         p_gather(i).start()
-
-    @pl.loop(0, GROUPS - 1)
-    def _(k):
-        for m in range(MEMBERS):
-            backward(k, m).start()
-
-    for m in range(1, MEMBERS):
-        backward(GROUPS - 1, m).start()
-    own_back = pltpu.make_async_copy(
-        back_send.at[GROUPS - 1, 0], back_recv.at[GROUPS - 1, 0], own_sem.at[1]
-    )
-    own_back.start()
 
     @pl.loop(0, D // 256)
     def _(i):
@@ -318,6 +326,7 @@
         moment_h[:, columns] = high
         moment_l[:, columns] = low
 
+    stores[1].start()
     for i in range(1, NDP):
         p_gather(i).wait_recv()
 
@@ -351,6 +360,7 @@
     three = jnp.concatenate([basis_h, basis_l, basis_h], axis=0).astype(F32)
     for i in range(FF // 128):
         factor_t[128 * i : 128 * i + 128, :] = three[:, 128 * i : 128 * i + 128].T.astype(BF16)
+    stores[2].start()
 
     for i in range(1, NDP):
         z_scatter(i).wait_recv()
@@ -370,26 +380,6 @@
     for i in range(1, NDP):
         q_gather(i).start()
 
-    def store(i):
-        block = pl.ds(pl.multiple_of(((replica + NDP - i) % NDP) * BLOCK, BLOCK), BLOCK)
-        return pltpu.make_async_copy(error_new.at[i], error_out.at[:, block], store_sem.at[i])
-
-    for i in (0, 1, 3, 2):
-        if i:
-            q_gather(i).wait_recv()
-        owner = (replica + NDP - i) % NDP
-        block = pl.ds(pl.multiple_of(owner * BLOCK, BLOCK), BLOCK)
-        part = q_full[owner]
-        q_out[:, block] = part
-        part_h, part_l = split(part)
-        part_three = jnp.concatenate([part_h, part_h, part_l], axis=0)
-        for j in range(3):
-            rows = slice(256 * j, 256 * j + 256)
-            error_new[i, rows, :] = (
-                moment[rows, block] - nn(factor_t[rows, :], part_three)
-            ).astype(BF16)
-        store(i).start()
-
     own_back.wait()
 
     @pl.loop(0, GROUPS - 1)
@@ -400,21 +390,14 @@
         main, tail = unpack(back_recv, k, FF, 3, 256)
         back_rows[rows, :] = jnp.concatenate([main, tail], axis=0)
 
-    for m in range(1, MEMBERS):
+    for m in range(MEMBERS - 1):
         backward(GROUPS - 1, m).wait_recv()
     main, tail = unpack(back_recv, GROUPS - 1, FF, 3, 256)
     back_rows[(GROUPS - 1) * GROUP_ROWS :, :] = jnp.concatenate([main, tail], axis=0)
-    for i in range(4):
-        chosen = lax.dot_general(
-            pick[:, 128 * i : 128 * i + 128],
-            back_rows[...],
-            (((0,), (0,)), ((), ())),
-            preferred_element_type=F32,
-        )
-        back_out[128 * i : 128 * i + 128, :] = chosen.astype(BF16)
-
-    for i in range(NDP):
-        store(i).wait()
+    for i in range(1, NDP):
+        q_gather(i).wait_recv()
+    for store in stores:
+        store.wait()
     for i in range(1, NDP):
         p_scatter(i).wait_send()
         p_gather(i).wait_send()
@@ -427,25 +410,42 @@
             forward(k, m).wait_send()
             backward(k, m).wait_send()
 
-    for m in range(1, MEMBERS):
+    for m in range(MEMBERS - 1):
         forward(GROUPS - 1, m).wait_send()
         backward(GROUPS - 1, m).wait_send()
+
+
+def finish(moment, factor_t, q_part, pick, back_rows, p_in, error_out, q_out, back_out, p_out):
+    part = q_part[0]
+    q_out[...] = part
+    p_out[...] = p_in[...]
+    high, low = split(part)
+    three = jnp.concatenate([high, high, low], axis=0)
+    for j in range(3):
+        rows = slice(256 * j, 256 * j + 256)
+        error_out[rows, :] = (moment[rows, :] - nn(factor_t[rows, :], three)).astype(BF16)
+    chosen = lax.dot_general(
+        pick[...], back_rows[...], (((0,), (0,)), ((), ())), preferred_element_type=F32
+    )
+    back_out[...] = chosen.astype(BF16)
 
 
 def shards(grad_rows, counts, order, hidden, down_weight, error_in, q_init):
     anywhere = pl.BlockSpec(memory_space=pl.ANY)
     vmem = pl.BlockSpec(memory_space=pltpu.VMEM)
     dma = pltpu.SemaphoreType.DMA
-    back, basis, factor, error_new = pl.pallas_call(
+    back_rows, basis, factor, moment, pick, factor_t = pl.pallas_call(
         kernel,
         out_shape=(
-            jax.ShapeDtypeStruct((ROWS, FF), BF16),
+            jax.ShapeDtypeStruct((640, FF), BF16),
             jax.ShapeDtypeStruct((RANK, FF), F32),
-            jax.ShapeDtypeStruct((RANK, D), F32),
-            jax.ShapeDtypeStruct((FF, D), BF16),
+            jax.ShapeDtypeStruct((NDP, RANK, BLOCK), F32),
+            jax.ShapeDtypeStruct((FF, D), F32),
+            jax.ShapeDtypeStruct((640, ROWS), BF16),
+            jax.ShapeDtypeStruct((FF, 3 * RANK), BF16),
         ),
         in_specs=[anywhere, vmem, vmem, anywhere, anywhere, anywhere, vmem],
-        out_specs=(vmem, vmem, vmem, anywhere),
+        out_specs=(vmem, vmem, vmem, anywhere, anywhere, anywhere),
         scratch_shapes=[
             pltpu.VMEM((ROWS, D), BF16),
             pltpu.VMEM((640, FF), BF16),
@@ -462,17 +462,14 @@
             pltpu.VMEM((640, ROWS), BF16),
             pltpu.VMEM((GROUPS, MEMBERS, 8, BACK), BF16),
             pltpu.VMEM((GROUPS, MEMBERS, 8, BACK), BF16),
-            pltpu.VMEM((640, FF), BF16),
             pltpu.VMEM((RANK, FF), F32),
             pltpu.VMEM((NDP - 1, P_ROWS, FF), F32),
             pltpu.VMEM((RANK, FF), F32),
             pltpu.VMEM((NDP, RANK, BLOCK), F32),
             pltpu.VMEM((NDP - 1, RANK, BLOCK), F32),
-            pltpu.VMEM((NDP, RANK, BLOCK), F32),
-            pltpu.VMEM((NDP, FF, BLOCK), BF16),
             pltpu.VMEM((FF, 3 * RANK), BF16),
             dma((4,)),
-            dma((NDP,)),
+            dma((3,)),
             dma((GROUPS, MEMBERS)),
             dma((GROUPS, MEMBERS)),
             dma((GROUPS, MEMBERS)),
@@ -496,7 +493,33 @@
         error_in[0, 0],
         q_init[0].T,
     )
-    return back[None], basis.T[None], factor.T[None], error_new[None, None]
+    error_new, q_out, back, p_out = pl.pallas_call(
+        finish,
+        grid=(NDP,),
+        out_shape=(
+            jax.ShapeDtypeStruct((FF, D), BF16),
+            jax.ShapeDtypeStruct((RANK, D), F32),
+            jax.ShapeDtypeStruct((ROWS, FF), BF16),
+            jax.ShapeDtypeStruct((RANK, FF), F32),
+        ),
+        in_specs=[
+            pl.BlockSpec((FF, BLOCK), lambda i: (0, i)),
+            pl.BlockSpec((FF, 3 * RANK), lambda i: (0, 0)),
+            pl.BlockSpec((1, RANK, BLOCK), lambda i: (i, 0, 0)),
+            pl.BlockSpec((640, ROWS // NDP), lambda i: (0, i)),
+            pl.BlockSpec((640, FF), lambda i: (0, 0)),
+            pl.BlockSpec((RANK, FF), lambda i: (0, 0)),
+        ],
+        out_specs=(
+            pl.BlockSpec((FF, BLOCK), lambda i: (0, i)),
+            pl.BlockSpec((RANK, BLOCK), lambda i: (0, i)),
+            pl.BlockSpec((ROWS // NDP, FF), lambda i: (i, 0)),
+            pl.BlockSpec((RANK, FF), lambda i: (0, 0)),
+        ),
+        compiler_params=pltpu.CompilerParams(vmem_limit_bytes=58 << 20),
+        name="finish",
+    )(moment, factor_t, factor, pick, back_rows, basis)
+    return back[None], p_out.T[None], q_out.T[None], error_new[None, None]
 
 
 def solution(mesh):

time: 126 us -> 108 us (0.86)
  local copies, waits for them, and re-layouts: 9.52 us -> 0 us
  Pallas kernels: 115 us -> 108 us
    unnamed x4 -> x0, local copies, waits for them, and re-layouts: 9.52 us -> none
    pallas_call x1 -> x2, Pallas kernels: 115 us -> 108 us  [the longest x1 101 us: shards(): pl.pallas_call(kernel, out_shape=(jax.ShapeDtypeStruct((640, FF), BF16),...]
where the time goes in v2:
time: 108 us
  Pallas kernels  108 us (100%)
    pallas_call x1, Pallas kernels, shards(): pl.pallas_call(kernel, out_shape=(jax.ShapeDtypeStruct((640, FF), BF16),...  101 us
    pallas_call x1, Pallas kernels, shards(): pl.pallas_call(finish, grid=(NDP,), out_shape=(jax.ShapeDtypeStruct((FF,...  6.7 us

profile of v2, /device:TPU:1, one launch (start us, length us, event | category | flops | bytes accessed | tf_op | source)
XLA Modules:
  0.0 108.2 jit_solution(13592290321930567053)
XLA Ops:
  0.6 100.9 %routed_backward.1 = (bf16[640,768]{1,0:T(8,128)(2,1)}, f32[64,768]{1,0:T(8,128)}, f32[4,64,512]{2,1,0:T(8,128)}, f32[768,2048]{1,0:T(8,128)}, bf16[640,512]{1,0:T(8,128)(2,1)}, /*index=5*/bf16[768,192]{1,0:T(8,128)(2,1)}) custom-call(bf16[512,2048]{1,0:T(8,128)(2,1)} %bitcast.18, s32[1,64]{1,0:T(1,128)} %bitcast.21, s32[1,512]{1,0:T(1,128)} %order_ref.1, ...), custom_call_target="tpu_custom_call" | custom-call | tf_op jit(solution)/shard_map/routed_backward/pallas_call | solution.py:437
  101.5 6.7 %finish.1 = (bf16[768,2048]{1,0:T(8,128)(2,1)}, f32[64,2048]{1,0:T(8,128)}, bf16[512,768]{1,0:T(8,128)(2,1)}, f32[64,768]{1,0:T(8,128)}) custom-call(f32[768,2048]{1,0:T(8,128)} %get-tuple-element.14.moment, bf16[768,192]{1,0:T(8,128)(2,1)} %get-tuple-element.15.factor_t, f32[4,64,512]{2,1,0:T(8,128)} %get-tuple-element.16.q_part, ...), custom_call_target="tpu_custom_call" | custom-call | tf_op jit(solution)/shard_map/finish/pallas_call | solution.py:496

commit v3 on v2

--- a/solution.py
+++ b/solution.py
@@ -17,6 +17,7 @@
 BACK = FF + 256
 BLOCK = D // NDP
 P_ROWS = RANK // NDP
+STEPS = 4
 
 
 def nn(a, b, precision=None):
@@ -77,15 +78,23 @@
     work = jnp.concatenate([gram, jnp.where(iota((RANK, RANK), 0) == iota((RANK, RANK), 1), 1.0, 0.0)], axis=1)
     blocks = [work[8 * b : 8 * b + 8] for b in range(8)]
     below = iota((8, 1), 0)
-    for k in range(RANK):
-        own, at = k // 8, k % 8
-        row = blocks[own][at : at + 1, :]
-        scaled = row / row[:, k : k + 1]
-        for b in range(own, 8):
-            factor = blocks[b][:, k : k + 1]
-            if b == own:
-                factor = jnp.where(below > at, factor, 0.0)
-            blocks[b] = blocks[b] - factor * scaled
+    for own in range(8):
+        columns = [
+            [jnp.broadcast_to(blocks[b][:, 8 * own + j : 8 * own + j + 1], (8, 2 * RANK)) for b in range(own, 8)]
+            for j in range(8)
+        ]
+        for j in range(8):
+            row = blocks[own][j : j + 1, :]
+            inverse = 1.0 / columns[j][0][j : j + 1, :]
+            scaled = row * inverse
+            for i in range(j + 1, 8):
+                across = columns[j][0][i : i + 1, :] * inverse
+                columns[i] = [there - here * across for there, here in zip(columns[i], columns[j])]
+            for b in range(own, 8):
+                factor = columns[j][b - own]
+                if b == own:
+                    factor = jnp.where(below > j, factor, 0.0)
+                blocks[b] = blocks[b] - factor * scaled
     work = jnp.concatenate(blocks, axis=0)
     pivots = jnp.sum(jnp.where(lanes == rows, work, 0.0), axis=1, keepdims=True)
     return work[:, RANK:] * lax.rsqrt(pivots)
@@ -93,9 +102,10 @@
 
 def kernel(
     x_hbm, counts_ref, order_ref, hidden_hbm, weight_hbm, error_hbm, q_ref,
-    back_rows, p_out, q_full, moment_out, pick_out, factor_out,
+    back_rows_out, p_out, q_full, moment_out, pick_out, factor_out,
     x, hidden, weight, error, send, recv, held, hidden_p, hidden_t, moment, moment_h, moment_l,
-    pick, back_send, back_recv, p_part, p_recv, p_full, z_part, z_recv, factor_t, load_sem, store_sem, send_sem, recv_sem, back_send_sem, back_recv_sem,
+    pick, back_send, back_recv, p_part, p_recv, p_full, z_part, z_recv, factor_t,
+    back_rows, basis_held, load_sem, store_sem, send_sem, recv_sem, back_send_sem, back_recv_sem,
     p_sem, g_sem, z_sem, q_sem, own_sem,
 ):
     me = lax.axis_index("expert")
@@ -201,14 +211,19 @@
         )
     wanted = routes(ends, order_ref[...].astype(F32))
 
+    places = []
     for k in range(GROUPS):
         main_code, tail_code = group_codes(y, z, c, k, 1, 16)
         code = jnp.concatenate([main_code, tail_code], axis=0).astype(F32)
-        pick[k * GROUP_ROWS : (k + 1) * GROUP_ROWS, :] = onehot(wanted == code)
+        places.append(jnp.where(wanted == code, 1.0, 0.0))
+    places = jnp.concatenate(places, axis=0)
+    for i in range(4):
+        pick[128 * i : 128 * i + 128, :] = places[:, 128 * i : 128 * i + 128].T.astype(BF16)
     stores = [
         pltpu.make_async_copy(src, dst, store_sem.at[i])
         for i, (src, dst) in enumerate(
-            [(pick, pick_out), (moment, moment_out), (factor_t, factor_out)]
+            [(pick, pick_out), (moment, moment_out), (factor_t, factor_out),
+             (basis_held, p_out), (back_rows, back_rows_out)]
         )
     ]
     stores[0].start()
@@ -355,7 +370,8 @@
     gram = nt(total, total, lax.Precision.HIGHEST)
     inverse = inverse_factor(gram)
     basis = nn(inverse, total, lax.Precision.HIGHEST)
-    p_out[...] = basis
+    basis_held[...] = basis
+    stores[3].start()
     basis_h, basis_l = split(basis)
     three = jnp.concatenate([basis_h, basis_l, basis_h], axis=0).astype(F32)
     for i in range(FF // 128):
@@ -394,6 +410,7 @@
         backward(GROUPS - 1, m).wait_recv()
     main, tail = unpack(back_recv, GROUPS - 1, FF, 3, 256)
     back_rows[(GROUPS - 1) * GROUP_ROWS :, :] = jnp.concatenate([main, tail], axis=0)
+    stores[4].start()
     for i in range(1, NDP):
         q_gather(i).wait_recv()
     for store in stores:
@@ -415,19 +432,23 @@
         backward(GROUPS - 1, m).wait_send()
 
 
-def finish(moment, factor_t, q_part, pick, back_rows, p_in, error_out, q_out, back_out, p_out):
-    part = q_part[0]
-    q_out[...] = part
-    p_out[...] = p_in[...]
-    high, low = split(part)
-    three = jnp.concatenate([high, high, low], axis=0)
-    for j in range(3):
-        rows = slice(256 * j, 256 * j + 256)
-        error_out[rows, :] = (moment[rows, :] - nn(factor_t[rows, :], three)).astype(BF16)
-    chosen = lax.dot_general(
-        pick[...], back_rows[...], (((0,), (0,)), ((), ())), preferred_element_type=F32
-    )
-    back_out[...] = chosen.astype(BF16)
+def finish(moment, factor_t, q_part, pick, back_rows, p_in, error_out, q_out, back_out, p_out, three):
+    @pl.when(pl.program_id(0) == 0)
+    def _():
+        p_out[...] = p_in[...]
+        for i in range(NDP):
+            part = q_part[i]
+            columns = slice(BLOCK * i, BLOCK * i + BLOCK)
+            q_out[:, columns] = part
+            high, low = split(part)
+            three[:, columns] = jnp.concatenate([high, high, low], axis=0)
+
+    for i in range(NDP):
+        columns = slice(BLOCK * i, BLOCK * i + BLOCK)
+        error_out[:, columns] = (
+            moment[:, columns] - nn(factor_t[...], three[:, columns])
+        ).astype(BF16)
+    back_out[...] = nn(pick[...], back_rows[...]).astype(BF16)
 
 
 def shards(grad_rows, counts, order, hidden, down_weight, error_in, q_init):
@@ -441,11 +462,11 @@
             jax.ShapeDtypeStruct((RANK, FF), F32),
             jax.ShapeDtypeStruct((NDP, RANK, BLOCK), F32),
             jax.ShapeDtypeStruct((FF, D), F32),
-            jax.ShapeDtypeStruct((640, ROWS), BF16),
+            jax.ShapeDtypeStruct((ROWS, 640), BF16),
             jax.ShapeDtypeStruct((FF, 3 * RANK), BF16),
         ),
         in_specs=[anywhere, vmem, vmem, anywhere, anywhere, anywhere, vmem],
-        out_specs=(vmem, vmem, vmem, anywhere, anywhere, anywhere),
+        out_specs=(anywhere, anywhere, vmem, anywhere, anywhere, anywhere),
         scratch_shapes=[
             pltpu.VMEM((ROWS, D), BF16),
             pltpu.VMEM((640, FF), BF16),
@@ -459,7 +480,7 @@
             pltpu.VMEM((FF, D), F32),
             pltpu.VMEM((FF, D), BF16),
             pltpu.VMEM((FF, D), BF16),
-            pltpu.VMEM((640, ROWS), BF16),
+            pltpu.VMEM((ROWS, 640), BF16),
             pltpu.VMEM((GROUPS, MEMBERS, 8, BACK), BF16),
             pltpu.VMEM((GROUPS, MEMBERS, 8, BACK), BF16),
             pltpu.VMEM((RANK, FF), F32),
@@ -468,8 +489,10 @@
             pltpu.VMEM((NDP, RANK, BLOCK), F32),
             pltpu.VMEM((NDP - 1, RANK, BLOCK), F32),
             pltpu.VMEM((FF, 3 * RANK), BF16),
+            pltpu.VMEM((640, FF), BF16),
+            pltpu.VMEM((RANK, FF), F32),
             dma((4,)),
-            dma((3,)),
+            dma((5,)),
             dma((GROUPS, MEMBERS)),
             dma((GROUPS, MEMBERS)),
             dma((GROUPS, MEMBERS)),
@@ -495,7 +518,7 @@
     )
     error_new, q_out, back, p_out = pl.pallas_call(
         finish,
-        grid=(NDP,),
+        grid=(STEPS,),
         out_shape=(
             jax.ShapeDtypeStruct((FF, D), BF16),
             jax.ShapeDtypeStruct((RANK, D), F32),
@@ -503,19 +526,20 @@
             jax.ShapeDtypeStruct((RANK, FF), F32),
         ),
         in_specs=[
-            pl.BlockSpec((FF, BLOCK), lambda i: (0, i)),
-            pl.BlockSpec((FF, 3 * RANK), lambda i: (0, 0)),
-            pl.BlockSpec((1, RANK, BLOCK), lambda i: (i, 0, 0)),
-            pl.BlockSpec((640, ROWS // NDP), lambda i: (0, i)),
+            pl.BlockSpec((FF // STEPS, D), lambda i: (i, 0)),
+            pl.BlockSpec((FF // STEPS, 3 * RANK), lambda i: (i, 0)),
+            pl.BlockSpec((NDP, RANK, BLOCK), lambda i: (0, 0, 0)),
+            pl.BlockSpec((ROWS // STEPS, 640), lambda i: (i, 0)),
             pl.BlockSpec((640, FF), lambda i: (0, 0)),
             pl.BlockSpec((RANK, FF), lambda i: (0, 0)),
         ],
         out_specs=(
-            pl.BlockSpec((FF, BLOCK), lambda i: (0, i)),
-            pl.BlockSpec((RANK, BLOCK), lambda i: (0, i)),
-            pl.BlockSpec((ROWS // NDP, FF), lambda i: (i, 0)),
+            pl.BlockSpec((FF // STEPS, D), lambda i: (i, 0)),
+            pl.BlockSpec((RANK, D), lambda i: (0, 0)),
+            pl.BlockSpec((ROWS // STEPS, FF), lambda i: (i, 0)),
             pl.BlockSpec((RANK, FF), lambda i: (0, 0)),
         ),
+        scratch_shapes=[pltpu.VMEM((3 * RANK, D), BF16)],
         compiler_params=pltpu.CompilerParams(vmem_limit_bytes=58 << 20),
         name="finish",
     )(moment, factor_t, factor, pick, back_rows, basis)

time: 108 us -> 109 us (level)
  no operation moved by 1% of the time
where the time goes in v3:
time: 109 us
  Pallas kernels  108 us (99%)
    pallas_call x1, Pallas kernels, shards(): pl.pallas_call(kernel, out_shape=(jax.ShapeDtypeStruct((640, FF), BF16),...  101 us
    pallas_call x1, Pallas kernels, shards(): pl.pallas_call(finish, grid=(STEPS,), out_shape=(jax.ShapeDtypeStruct((FF...  6.76 us

profile of v3, /device:TPU:1, one launch (start us, length us, event | category | flops | bytes accessed | tf_op | source)
XLA Modules:
  0.0 108.9 jit_solution(13138927807499167307)
XLA Ops:
  0.6 101.5 %routed_backward.1 = (bf16[640,768]{1,0:T(8,128)(2,1)}, f32[64,768]{1,0:T(8,128)}, f32[4,64,512]{2,1,0:T(8,128)}, f32[768,2048]{1,0:T(8,128)}, bf16[512,640]{1,0:T(8,128)(2,1)}, /*index=5*/bf16[768,192]{1,0:T(8,128)(2,1)}) custom-call(bf16[512,2048]{1,0:T(8,128)(2,1)} %bitcast.18, s32[1,64]{1,0:T(1,128)} %bitcast.21, s32[1,512]{1,0:T(1,128)} %order_ref.1, ...), custom_call_target="tpu_custom_call" | custom-call | tf_op jit(solution)/shard_map/routed_backward/pallas_call | solution.py:458
  102.1 6.8 %finish.1 = (bf16[768,2048]{1,0:T(8,128)(2,1)}, f32[64,2048]{1,0:T(8,128)}, bf16[512,768]{1,0:T(8,128)(2,1)}, f32[64,768]{1,0:T(8,128)}) custom-call(f32[768,2048]{1,0:T(8,128)} %get-tuple-element.14.moment, bf16[768,192]{1,0:T(8,128)(2,1)} %get-tuple-element.15.factor_t, f32[4,64,512]{2,1,0:T(8,128)} %get-tuple-element.16.q_part, ...), custom_call_target="tpu_custom_call" | custom-call | tf_op jit(solution)/shard_map/finish/pallas_call | solution.py:519

commit v4 on v3

--- a/solution.py
+++ b/solution.py
@@ -16,6 +16,7 @@
 WIDE = D + 512
 BACK = FF + 256
 BLOCK = D // NDP
+HALF = BLOCK // 2
 P_ROWS = RANK // NDP
 STEPS = 4
 
@@ -349,23 +350,24 @@
     total_h, total_l = split(total)
     total_both = jnp.concatenate([total_h, total_l], axis=0)
 
-    def z_scatter(i):
+    def z_scatter(h, i):
         peer = (replica + i) % NDP
         return pltpu.make_async_remote_copy(
-            src_ref=z_part.at[i],
-            dst_ref=z_recv.at[i - 1],
-            send_sem=z_sem.at[0, i - 1],
-            recv_sem=z_sem.at[1, i - 1],
+            src_ref=z_part.at[h, i],
+            dst_ref=z_recv.at[h, i - 1],
+            send_sem=z_sem.at[h, 0, i - 1],
+            recv_sem=z_sem.at[h, 1, i - 1],
             device_id={"dp": peer},
             device_id_type=MESH,
         )
 
-    for i in (2, 1, 3, 0):
-        block = pl.ds(pl.multiple_of(((replica + i) % NDP) * BLOCK, BLOCK), BLOCK)
+    for h, i in ((0, 2), (0, 1), (0, 3), (1, 2), (1, 1), (1, 3), (0, 0), (1, 0)):
+        start = ((replica + i) % NDP) * BLOCK + h * HALF
+        block = pl.ds(pl.multiple_of(start, HALF), HALF)
         both = nn(total_both, moment_h[:, block])
-        z_part[i] = both[:RANK] + both[RANK:] + nn(total_h, moment_l[:, block])
+        z_part[h, i] = both[:RANK] + both[RANK:] + nn(total_h, moment_l[:, block])
         if i:
-            z_scatter(i).start()
+            z_scatter(h, i).start()
 
     gram = nt(total, total, lax.Precision.HIGHEST)
     inverse = inverse_factor(gram)
@@ -378,23 +380,23 @@
         factor_t[128 * i : 128 * i + 128, :] = three[:, 128 * i : 128 * i + 128].T.astype(BF16)
     stores[2].start()
 
-    for i in range(1, NDP):
-        z_scatter(i).wait_recv()
-    z_total = z_part[0] + z_recv[0] + z_recv[1] + z_recv[2]
-    q_full[replica] = nn(inverse, z_total, lax.Precision.HIGHEST) / NDP
-
-    def q_gather(i):
+    def q_gather(h, i):
         return pltpu.make_async_remote_copy(
-            src_ref=q_full.at[replica],
-            dst_ref=q_full.at[replica],
-            send_sem=q_sem.at[0, i - 1],
-            recv_sem=q_sem.at[1, i - 1],
+            src_ref=q_full.at[replica, h],
+            dst_ref=q_full.at[replica, h],
+            send_sem=q_sem.at[h, 0, i - 1],
+            recv_sem=q_sem.at[h, 1, i - 1],
             device_id={"dp": (replica + i) % NDP},
             device_id_type=MESH,
         )
 
-    for i in range(1, NDP):
-        q_gather(i).start()
+    for h in range(2):
+        for i in range(1, NDP):
+            z_scatter(h, i).wait_recv()
+        z_total = z_part[h, 0] + z_recv[h, 0] + z_recv[h, 1] + z_recv[h, 2]
+        q_full[replica, h] = nn(inverse, z_total, lax.Precision.HIGHEST) / NDP
+        for i in (2, 1, 3):
+            q_gather(h, i).start()
 
     own_back.wait()
 
@@ -412,14 +414,16 @@
     back_rows[(GROUPS - 1) * GROUP_ROWS :, :] = jnp.concatenate([main, tail], axis=0)
     stores[4].start()
     for i in range(1, NDP):
-        q_gather(i).wait_recv()
+        q_gather(0, i).wait_recv()
+        q_gather(1, i).wait_recv()
     for store in stores:
         store.wait()
     for i in range(1, NDP):
         p_scatter(i).wait_send()
         p_gather(i).wait_send()
-        z_scatter(i).wait_send()
-        q_gather(i).wait_send()
+        for h in range(2):
+            z_scatter(h, i).wait_send()
+            q_gather(h, i).wait_send()
 
     @pl.loop(0, GROUPS - 1)
     def _(k):
@@ -436,9 +440,9 @@
     @pl.when(pl.program_id(0) == 0)
     def _():
         p_out[...] = p_in[...]
-        for i in range(NDP):
-            part = q_part[i]
-            columns = slice(BLOCK * i, BLOCK * i + BLOCK)
+        for i in range(2 * NDP):
+            part = q_part[i // 2, i % 2]
+            columns = slice(HALF * i, HALF * i + HALF)
             q_out[:, columns] = part
             high, low = split(part)
             three[:, columns] = jnp.concatenate([high, high, low], axis=0)
@@ -460,7 +464,7 @@
         out_shape=(
             jax.ShapeDtypeStruct((640, FF), BF16),
             jax.ShapeDtypeStruct((RANK, FF), F32),
-            jax.ShapeDtypeStruct((NDP, RANK, BLOCK), F32),
+            jax.ShapeDtypeStruct((NDP, 2, RANK, HALF), F32),
             jax.ShapeDtypeStruct((FF, D), F32),
             jax.ShapeDtypeStruct((ROWS, 640), BF16),
             jax.ShapeDtypeStruct((FF, 3 * RANK), BF16),
@@ -486,8 +490,8 @@
             pltpu.VMEM((RANK, FF), F32),
             pltpu.VMEM((NDP - 1, P_ROWS, FF), F32),
             pltpu.VMEM((RANK, FF), F32),
-            pltpu.VMEM((NDP, RANK, BLOCK), F32),
-            pltpu.VMEM((NDP - 1, RANK, BLOCK), F32),
+            pltpu.VMEM((2, NDP, RANK, HALF), F32),
+            pltpu.VMEM((2, NDP - 1, RANK, HALF), F32),
             pltpu.VMEM((FF, 3 * RANK), BF16),
             pltpu.VMEM((640, FF), BF16),
             pltpu.VMEM((RANK, FF), F32),
@@ -499,8 +503,8 @@
             dma((GROUPS, MEMBERS)),
             dma((2, NDP - 1)),
             dma((2, NDP - 1)),
-            dma((2, NDP - 1)),
-            dma((2, NDP - 1)),
+            dma((2, 2, NDP - 1)),
+            dma((2, 2, NDP - 1)),
             dma((2,)),
         ],
         compiler_params=pltpu.CompilerParams(
@@ -528,7 +532,7 @@
         in_specs=[
             pl.BlockSpec((FF // STEPS, D), lambda i: (i, 0)),
             pl.BlockSpec((FF // STEPS, 3 * RANK), lambda i: (i, 0)),
-            pl.BlockSpec((NDP, RANK, BLOCK), lambda i: (0, 0, 0)),
+            pl.BlockSpec((NDP, 2, RANK, HALF), lambda i: (0, 0, 0, 0)),
             pl.BlockSpec((ROWS // STEPS, 640), lambda i: (i, 0)),
             pl.BlockSpec((640, FF), lambda i: (0, 0)),
             pl.BlockSpec((RANK, FF), lambda i: (0, 0)),

time: 109 us -> 109 us (level)
  no operation moved by 1% of the time
where the time goes in v4:
time: 109 us
  Pallas kernels  108 us (99%)
    pallas_call x1, Pallas kernels, shards(): pl.pallas_call(kernel, out_shape=(jax.ShapeDtypeStruct((640, FF), BF16),...  102 us
    pallas_call x1, Pallas kernels, shards(): pl.pallas_call(finish, grid=(STEPS,), out_shape=(jax.ShapeDtypeStruct((FF...  6.77 us

profile of v4, /device:TPU:1, one launch (start us, length us, event | category | flops | bytes accessed | tf_op | source)
XLA Modules:
  0.0 109.0 jit_solution(3178077122308370556)
XLA Ops:
  0.6 101.6 %routed_backward.1 = (bf16[640,768]{1,0:T(8,128)(2,1)}, f32[64,768]{1,0:T(8,128)}, f32[4,2,64,256]{3,2,1,0:T(8,128)}, f32[768,2048]{1,0:T(8,128)}, bf16[512,640]{1,0:T(8,128)(2,1)}, /*index=5*/bf16[768,192]{1,0:T(8,128)(2,1)}) custom-call(bf16[512,2048]{1,0:T(8,128)(2,1)} %bitcast.18, s32[1,64]{1,0:T(1,128)} %bitcast.21, s32[1,512]{1,0:T(1,128)} %order_ref.1, ...), custom_call_target="tpu_custom_call" | custom-call | tf_op jit(solution)/shard_map/routed_backward/pallas_call | solution.py:462
  102.2 6.8 %finish.1 = (bf16[768,2048]{1,0:T(8,128)(2,1)}, f32[64,2048]{1,0:T(8,128)}, bf16[512,768]{1,0:T(8,128)(2,1)}, f32[64,768]{1,0:T(8,128)}) custom-call(f32[768,2048]{1,0:T(8,128)} %get-tuple-element.14.moment, bf16[768,192]{1,0:T(8,128)(2,1)} %get-tuple-element.15.factor_t, f32[4,2,64,256]{3,2,1,0:T(8,128)} %get-tuple-element.16.q_part, ...), custom_call_target="tpu_custom_call" | custom-call | tf_op jit(solution)/shard_map/finish/pallas_call | solution.py:523

commit v5 on v4

--- a/solution.py
+++ b/solution.py
@@ -19,6 +19,7 @@
 HALF = BLOCK // 2
 P_ROWS = RANK // NDP
 STEPS = 4
+EARLY = 2
 
 
 def nn(a, b, precision=None):
@@ -275,12 +276,21 @@
                 total = total + placed
         back_send[k, :, :, FF:] = total.reshape(8, 8, 256).astype(BF16)
 
-    @pl.loop(0, GROUPS - 1)
+    @pl.loop(0, GROUPS - 1 - EARLY)
     def _(k):
         for m in range(MEMBERS):
             forward(k, m).wait_recv()
         take(k)
         answer(k)
+
+    @pl.loop(GROUPS - 1 - EARLY, GROUPS - 1)
+    def _(k):
+        for m in range(MEMBERS):
+            forward(k, m).wait_recv()
+        take(k)
+        answer(k)
+        for m in range(MEMBERS):
+            backward(k - (GROUPS - 1 - EARLY), m).start()
 
     for m in range(MEMBERS - 1):
         forward(GROUPS - 1, m).wait_recv()
@@ -313,7 +323,7 @@
     for i in range(1, NDP):
         p_scatter(i).start()
 
-    @pl.loop(0, GROUPS - 1)
+    @pl.loop(EARLY, GROUPS - 1)
     def _(k):
         for m in range(MEMBERS):
             backward(k, m).start()

time: 109 us -> 107 us (0.982)
  Pallas kernels: 108 us -> 106 us
    pallas_call x1, Pallas kernels: 102 us -> 99.1 us  [shards(): pl.pallas_call(kernel, out_shape=(jax.ShapeDtypeStruct((640, FF), BF16),...]
where the time goes in v5:
time: 107 us; the launch traced here: 106 us
  Pallas kernels  106 us (99%)
    pallas_call x1, Pallas kernels, shards(): pl.pallas_call(kernel, out_shape=(jax.ShapeDtypeStruct((640, FF), BF16),...  99.1 us
    pallas_call x1, Pallas kernels, shards(): pl.pallas_call(finish, grid=(STEPS,), out_shape=(jax.ShapeDtypeStruct((FF...  6.77 us

profile of v5, /device:TPU:1, one launch (start us, length us, event | category | flops | bytes accessed | tf_op | source)
XLA Modules:
  0.0 106.5 jit_solution(14921041932016982108)
XLA Ops:
  0.6 99.1 %routed_backward.1 = (bf16[640,768]{1,0:T(8,128)(2,1)}, f32[64,768]{1,0:T(8,128)}, f32[4,2,64,256]{3,2,1,0:T(8,128)}, f32[768,2048]{1,0:T(8,128)}, bf16[512,640]{1,0:T(8,128)(2,1)}, /*index=5*/bf16[768,192]{1,0:T(8,128)(2,1)}) custom-call(bf16[512,2048]{1,0:T(8,128)(2,1)} %bitcast.18, s32[1,64]{1,0:T(1,128)} %bitcast.21, s32[1,512]{1,0:T(1,128)} %order_ref.1, ...), custom_call_target="tpu_custom_call" | custom-call | tf_op jit(solution)/shard_map/routed_backward/pallas_call | solution.py:472
  99.7 6.8 %finish.1 = (bf16[768,2048]{1,0:T(8,128)(2,1)}, f32[64,2048]{1,0:T(8,128)}, bf16[512,768]{1,0:T(8,128)(2,1)}, f32[64,768]{1,0:T(8,128)}) custom-call(f32[768,2048]{1,0:T(8,128)} %get-tuple-element.14.moment, bf16[768,192]{1,0:T(8,128)(2,1)} %get-tuple-element.15.factor_t, f32[4,2,64,256]{3,2,1,0:T(8,128)} %get-tuple-element.16.q_part, ...), custom_call_target="tpu_custom_call" | custom-call | tf_op jit(solution)/shard_map/finish/pallas_call | solution.py:533
